TPU v7x, 32 devices: a whole 2x2x4 slice. The times are simulated.
32 devices in a mesh: dp: 16 (over z, y, x), tensor: 2 (over core).
Axes of the slice: x: 2, y: 2, z: 4, core: 2. Of those that a mesh axis runs over, the one named last changes fastest.
Arguments:
- tokens_in: bfloat16 [4096, 1536], P('dp'), may hold values from -6 to 6
- seq_lengths: int32 [16, 16], P('dp'), may hold values from 0 to 256, as said below
- gain_attn: bfloat16 [1536], P('dp'), may hold values from 0.099609375 to 1.8984375
- w_query: bfloat16 [1536, 1536], P(('tensor', 'dp')), may hold values from -3 to 3
- b_query: bfloat16 [1536], P(('tensor', 'dp')), may hold values from -3 to 3
- w_key: bfloat16 [256, 1536], P(('tensor', 'dp')), may hold values from -3 to 3
- b_key: bfloat16 [256], P(('tensor', 'dp')), may hold values from -3 to 3
- w_value: bfloat16 [256, 1536], P(('tensor', 'dp')), may hold values from -0.15625 to 0.15625
- b_value: bfloat16 [256], P(('tensor', 'dp')), may hold values from -3 to 3
- w_out: bfloat16 [1536, 1536], P(('tensor', 'dp')), may hold values from -0.625 to 0.625
- gain_mlp: bfloat16 [1536], P('dp'), may hold values from 0.099609375 to 1.8984375
- w_gate: bfloat16 [8960, 1536], P(('tensor', 'dp')), may hold values from -0.15625 to 0.15625
- w_up: bfloat16 [8960, 1536], P(('tensor', 'dp')), may hold values from -0.15625 to 0.15625
- w_down: bfloat16 [8960, 1536], P(('tensor', 'dp')), may hold values from -0.125 to 0.125
- grad_out: bfloat16 [4096, 1536], P('dp'), may hold values from -6 to 6
Outputs:
- block_out: float32 [4096, 1536], P('dp')
- grad_in: float32 [4096, 1536], P('dp')
- grad_gain_attn: float32 [1536], P('dp')
- grad_w_query: float32 [1536, 1536], P(('tensor', 'dp'))
- grad_b_query: float32 [1536], P(('tensor', 'dp'))
- grad_w_key: float32 [256, 1536], P(('tensor', 'dp'))
- grad_b_key: float32 [256], P('tensor')
- grad_w_value: float32 [256, 1536], P(('tensor', 'dp'))
- grad_b_value: float32 [256], P(('tensor', 'dp'))
- grad_w_out: float32 [1536, 1536], P(('tensor', 'dp'))
- grad_gain_mlp: float32 [1536], P('dp')
- grad_w_gate: float32 [8960, 1536], P(('tensor', 'dp'))
- grad_w_up: float32 [8960, 1536], P(('tensor', 'dp'))
- grad_w_down: float32 [8960, 1536], P(('tensor', 'dp'))
Inputs may be any that keep to these rules, and one draw needn't show every extreme that they name: `seq_lengths`: row r lists, in order, the lengths of the sequences packed in tokens r * 256 to (r + 1) * 256 - 1: they sum to 256, live slots come first and are 1 or more, unused slots are 0, and some row holds a single sequence of 256 tokens.
All inputs are finite; a program needn't handle non-finite values.
Results may differ from a plain program's by a relative error of at most 0.023.
Values may be sent and summed in bfloat16 or wider, within the bound.
No kernel may reach another device: no remote copies, remote signals or barrier semaphores. Data moves between devices by JAX's collectives and lax.ppermute only.
A program may use at most 256 MiB of HBM per device.

v0:
```python
import math
import jax
import jax.numpy as jnp
from jax import lax
from jax.sharding import PartitionSpec as P

H = 12
KVH = 2
HD = 128
EPSILON = 1e-06
ROPE_BASE = 1000000.0
BLOCK_LIMIT = 512


def packed_layout(seq_lengths, row_tokens):
    ends_all = jnp.cumsum(seq_lengths, axis=1)
    places = jnp.arange(row_tokens, dtype=jnp.int32)
    passed = ends_all[:, None, :] <= places[None, :, None]
    segment = jnp.sum(passed.astype(jnp.int32), axis=2)
    opening = jnp.sum(jnp.where(passed, seq_lengths[:, None, :], 0), axis=2)
    return (segment, places[None, :] - opening)


def rope_tables(positions):
    half_size = HD // 2
    frequency = ROPE_BASE ** (-(jnp.arange(half_size, dtype=jnp.float32) * 2.0) / HD)
    angles = positions.astype(jnp.float32)[:, None] * frequency[None, :]
    cosine = jnp.cos(angles)
    sine_table = jnp.sin(angles)
    return (
        jnp.concatenate([cosine, cosine], axis=1),
        jnp.concatenate([sine_table, sine_table], axis=1),
    )


def rotate(vectors, cosine, sine_table):
    half_size = vectors.shape[-1] // 2
    turned = jnp.concatenate([-vectors[..., half_size:], vectors[..., :half_size]], axis=-1)
    return vectors * cosine[:, None, :] + turned * sine_table[:, None, :]


def unrotate(gradient, cosine, sine_table):
    half_size = gradient.shape[-1] // 2
    scaled = gradient * sine_table[:, None, :]
    turned = jnp.concatenate([scaled[..., half_size:], -scaled[..., :half_size]], axis=-1)
    return gradient * cosine[:, None, :] + turned


def inverse_rms(values):
    return lax.rsqrt(jnp.mean(values * values, axis=1, keepdims=True) + EPSILON)


def project(left_side, weight):
    return jnp.einsum("td,fd->tf", left_side, weight, preferred_element_type=jnp.float32)


def contract(left_side, right_side):
    return lax.dot_general(
        left_side, right_side, (((0,), (0,)), ((), ())), preferred_element_type=jnp.float32
    )


def masked_scores(query_block, keys_rot, allowed, score_scale):
    scores = (
        jnp.einsum("qkgd,tkd->kgqt", query_block, keys_rot, preferred_element_type=jnp.float32)
        * score_scale
    )
    return jnp.where(allowed[None, None], scores, -jnp.inf)


def shards(
    tokens_in,
    seq_lengths,
    gain_attn,
    w_query,
    b_query,
    w_key,
    b_key,
    w_value,
    b_value,
    w_out,
    gain_mlp,
    w_gate,
    w_up,
    w_down,
    grad_out,
):
    row_tokens = tokens_in.shape[0]
    group_heads = H // KVH
    score_scale = 1.0 / math.sqrt(HD)
    segments, positions = packed_layout(seq_lengths, row_tokens)
    segment = segments[0]
    cosine, sine_table = rope_tables(positions[0])
    places = jnp.arange(row_tokens, dtype=jnp.int32)
    block_rows = min(row_tokens, BLOCK_LIMIT)
    block_count = row_tokens // block_rows
    segment_blocks = segment.reshape(block_count, block_rows)
    place_blocks = places.reshape(block_count, block_rows)

    def block_mask(segment_block, place_block):
        return (segment_block[:, None] == segment[None, :]) & (
            place_block[:, None] >= places[None, :]
        )

    gathered = (
        lax.all_gather(gain_attn, "dp", axis=0, tiled=True),
        lax.all_gather(w_query, "dp", axis=0, tiled=True),
        lax.all_gather(b_query, "dp", axis=0, tiled=True),
        lax.all_gather(w_key, "dp", axis=0, tiled=True),
        lax.all_gather(b_key, "dp", axis=0, tiled=True),
        lax.all_gather(w_value, "dp", axis=0, tiled=True),
        lax.all_gather(b_value, "dp", axis=0, tiled=True),
        lax.all_gather(w_out, "dp", axis=0, tiled=True),
        lax.all_gather(gain_mlp, "dp", axis=0, tiled=True),
    )
    (
        gain_first,
        query_weight,
        query_bias,
        key_weight,
        key_bias,
        value_weight,
        value_bias,
        out_weight,
        gain_second,
    ) = gathered
    query_heads = query_weight.shape[0] // HD
    key_heads = key_weight.shape[0] // HD
    inputs = tokens_in.astype(jnp.float32)
    inverse_first = inverse_rms(inputs)
    normed_first = inputs * inverse_first
    first_low = (normed_first * gain_first.astype(jnp.float32)).astype(jnp.bfloat16)
    query_pre = project(first_low, query_weight) + query_bias.astype(jnp.float32)
    keys_pre = project(first_low, key_weight) + key_bias.astype(jnp.float32)
    values_pre = project(first_low, value_weight) + value_bias.astype(jnp.float32)
    query_rot = rotate(query_pre.reshape(row_tokens, query_heads, HD), cosine, sine_table).astype(
        jnp.bfloat16
    )
    keys_rot = rotate(keys_pre.reshape(row_tokens, key_heads, HD), cosine, sine_table).astype(
        jnp.bfloat16
    )
    values_low = values_pre.reshape(row_tokens, key_heads, HD).astype(jnp.bfloat16)
    query_blocks = query_rot.reshape(block_count, block_rows, key_heads, group_heads, HD)

    def forward_block(operands):
        query_block, segment_block, place_block = operands
        scores = masked_scores(
            query_block, keys_rot, block_mask(segment_block, place_block), score_scale
        )
        largest = jnp.max(scores, axis=3, keepdims=True)
        log_total = largest + jnp.log(jnp.sum(jnp.exp(scores - largest), axis=3, keepdims=True))
        probability = jnp.exp(scores - log_total).astype(jnp.bfloat16)
        attended_block = jnp.einsum(
            "kgqt,tkd->qkgd", probability, values_low, preferred_element_type=jnp.float32
        )
        return (attended_block.astype(jnp.bfloat16), log_total)

    attended_blocks, log_totals = lax.map(
        forward_block, (query_blocks, segment_blocks, place_blocks)
    )
    attended = attended_blocks.reshape(row_tokens, query_heads * HD)
    attn_part = jnp.dot(attended, out_weight, preferred_element_type=jnp.float32)
    hidden_state = inputs + lax.psum(attn_part, "tensor")
    inverse_second = inverse_rms(hidden_state)
    normed_second = hidden_state * inverse_second
    second_low = (normed_second * gain_second.astype(jnp.float32)).astype(jnp.bfloat16)
    piece_gate = lax.all_gather(w_gate, "dp", axis=0, tiled=True)
    piece_up = lax.all_gather(w_up, "dp", axis=0, tiled=True)
    piece_down = lax.all_gather(w_down, "dp", axis=0, tiled=True)
    gate_vals = project(second_low, piece_gate)
    up_vals = project(second_low, piece_up)
    hidden_low = (jax.nn.silu(gate_vals) * up_vals).astype(jnp.bfloat16)
    mlp_part = jnp.dot(hidden_low, piece_down, preferred_element_type=jnp.float32)
    block_out = hidden_state + lax.psum(mlp_part.astype(jnp.bfloat16), "tensor").astype(jnp.float32)
    piece_gate = lax.all_gather(w_gate, "dp", axis=0, tiled=True)
    piece_up = lax.all_gather(w_up, "dp", axis=0, tiled=True)
    piece_down = lax.all_gather(w_down, "dp", axis=0, tiled=True)
    gate_vals = project(second_low, piece_gate)
    up_vals = project(second_low, piece_up)
    sigmoid_vals = jax.nn.sigmoid(gate_vals)
    silu_vals = jax.nn.silu(gate_vals)
    hidden_low = (silu_vals * up_vals).astype(jnp.bfloat16)
    grad_hidden = project(grad_out, piece_down)
    grad_gate = (
        grad_hidden * up_vals * (sigmoid_vals * (1.0 + gate_vals * (1.0 - sigmoid_vals)))
    ).astype(jnp.bfloat16)
    grad_up = (grad_hidden * silu_vals).astype(jnp.bfloat16)
    grad_second = jnp.dot(grad_gate, piece_gate, preferred_element_type=jnp.float32) + jnp.dot(
        grad_up, piece_up, preferred_element_type=jnp.float32
    )
    gate_grads = grad_gate
    up_grads = grad_up
    hidden_all = hidden_low
    grad_second, gate_grads, up_grads, hidden_all = (grad_second, gate_grads, up_grads, hidden_all)
    grad_second = lax.psum(grad_second, "tensor")
    traded = (
        lax.all_to_all(gate_grads, "dp", split_axis=1, concat_axis=0, tiled=True),
        lax.all_to_all(up_grads, "dp", split_axis=1, concat_axis=0, tiled=True),
        lax.all_to_all(hidden_all, "dp", split_axis=1, concat_axis=0, tiled=True),
    )
    piece_second = lax.all_gather(second_low, "dp", axis=0, tiled=True)
    piece_grad = lax.all_gather(grad_out, "dp", axis=0, tiled=True)
    gate_rows = traded[0]
    up_rows = traded[1]
    hidden_rows = traded[2]
    grad_w_gate = contract(gate_rows, piece_second)
    grad_w_up = contract(up_rows, piece_second)
    grad_w_down = contract(hidden_rows, piece_grad)
    grad_gain_second = jnp.sum(grad_second * normed_second, axis=0)
    scaled_second = grad_second * gain_second.astype(jnp.float32)
    grad_hidden_state = grad_out.astype(jnp.float32) + inverse_second * (
        scaled_second
        - normed_second * jnp.mean(scaled_second * normed_second, axis=1, keepdims=True)
    )
    grad_branch = grad_hidden_state.astype(jnp.bfloat16)
    back_first, back_query, back_key, back_value, back_out = (
        lax.all_gather(gain_attn, "dp", axis=0, tiled=True),
        lax.all_gather(w_query, "dp", axis=0, tiled=True),
        lax.all_gather(w_key, "dp", axis=0, tiled=True),
        lax.all_gather(w_value, "dp", axis=0, tiled=True),
        lax.all_gather(w_out, "dp", axis=0, tiled=True),
    )
    grad_out_weight = contract(attended, grad_branch)
    grad_attended = project(grad_branch, back_out).astype(jnp.bfloat16)
    grad_blocks = grad_attended.reshape(block_count, block_rows, key_heads, group_heads, HD)

    def backward_block(operands):
        query_block, segment_block, place_block, log_total, grad_block = operands
        scores = masked_scores(
            query_block, keys_rot, block_mask(segment_block, place_block), score_scale
        )
        probability = jnp.exp(scores - log_total)
        grad_prob = jnp.einsum(
            "qkgd,tkd->kgqt", grad_block, values_low, preferred_element_type=jnp.float32
        )
        weighted = jnp.sum(probability * grad_prob, axis=3, keepdims=True)
        grad_scores = (probability * (grad_prob - weighted)).astype(jnp.bfloat16)
        grad_query = (
            jnp.einsum("kgqt,tkd->qkgd", grad_scores, keys_rot, preferred_element_type=jnp.float32)
            * score_scale
        )
        grad_keys = (
            jnp.einsum(
                "kgqt,qkgd->tkd", grad_scores, query_block, preferred_element_type=jnp.float32
            )
            * score_scale
        )
        grad_values = jnp.einsum(
            "kgqt,qkgd->tkd",
            probability.astype(jnp.bfloat16),
            grad_block,
            preferred_element_type=jnp.float32,
        )
        return (grad_query, grad_keys, grad_values)

    query_parts, key_parts, value_parts = lax.map(
        backward_block, (query_blocks, segment_blocks, place_blocks, log_totals, grad_blocks)
    )
    grad_query_low = (
        unrotate(query_parts.reshape(row_tokens, query_heads, HD), cosine, sine_table)
        .reshape(row_tokens, query_heads * HD)
        .astype(jnp.bfloat16)
    )
    grad_keys_low = (
        unrotate(jnp.sum(key_parts, axis=0), cosine, sine_table)
        .reshape(row_tokens, key_heads * HD)
        .astype(jnp.bfloat16)
    )
    grad_values_low = (
        jnp.sum(value_parts, axis=0).reshape(row_tokens, key_heads * HD).astype(jnp.bfloat16)
    )
    grad_query_weight = contract(grad_query_low, first_low)
    grad_query_bias = jnp.sum(grad_query_low, axis=0, dtype=jnp.float32)
    grad_key_weight = contract(grad_keys_low, first_low)
    grad_key_bias = jnp.sum(grad_keys_low, axis=0, dtype=jnp.float32)
    grad_value_weight = contract(grad_values_low, first_low)
    grad_value_bias = jnp.sum(grad_values_low, axis=0, dtype=jnp.float32)
    key_bias_total = lax.psum(grad_key_bias, "dp")
    grad_first = jnp.dot(grad_query_low, back_query, preferred_element_type=jnp.float32)
    grad_first = grad_first + jnp.dot(grad_keys_low, back_key, preferred_element_type=jnp.float32)
    grad_first = grad_first + jnp.dot(
        grad_values_low, back_value, preferred_element_type=jnp.float32
    )
    grad_first = lax.psum(grad_first.astype(jnp.bfloat16), "tensor").astype(jnp.float32)
    grad_gain_first = jnp.sum(grad_first * normed_first, axis=0)
    scaled_first = grad_first * back_first.astype(jnp.float32)
    grad_in = grad_hidden_state + inverse_first * (
        scaled_first - normed_first * jnp.mean(scaled_first * normed_first, axis=1, keepdims=True)
    )
    summed = (
        lax.psum_scatter(grad_gain_first, "dp", scatter_dimension=0, tiled=True),
        lax.psum_scatter(grad_query_weight, "dp", scatter_dimension=0, tiled=True),
        lax.psum_scatter(grad_query_bias, "dp", scatter_dimension=0, tiled=True),
        lax.psum_scatter(grad_key_weight, "dp", scatter_dimension=0, tiled=True),
        lax.psum_scatter(grad_value_weight, "dp", scatter_dimension=0, tiled=True),
        lax.psum_scatter(grad_value_bias, "dp", scatter_dimension=0, tiled=True),
        lax.psum_scatter(grad_out_weight, "dp", scatter_dimension=0, tiled=True),
        lax.psum_scatter(grad_gain_second, "dp", scatter_dimension=0, tiled=True),
    )
    return (
        block_out,
        grad_in,
        summed[0],
        summed[1],
        summed[2],
        summed[3],
        key_bias_total,
        summed[4],
        summed[5],
        summed[6],
        summed[7],
        grad_w_gate,
        grad_w_up,
        grad_w_down,
    )


def solution(mesh):
    in_specs = (
        P("dp", None),
        P("dp", None),
        P("dp"),
        P(("tensor", "dp"), None),
        P(("tensor", "dp")),
        P(("tensor", "dp"), None),
        P(("tensor", "dp")),
        P(("tensor", "dp"), None),
        P(("tensor", "dp")),
        P(("tensor", "dp"), None),
        P("dp"),
        P(("tensor", "dp"), None),
        P(("tensor", "dp"), None),
        P(("tensor", "dp"), None),
        P("dp", None),
    )
    out_specs = (
        P("dp", None),
        P("dp", None),
        P("dp"),
        P(("tensor", "dp"), None),
        P(("tensor", "dp")),
        P(("tensor", "dp"), None),
        P("tensor"),
        P(("tensor", "dp"), None),
        P(("tensor", "dp")),
        P(("tensor", "dp"), None),
        P("dp"),
        P(("tensor", "dp"), None),
        P(("tensor", "dp"), None),
        P(("tensor", "dp"), None),
    )
    return jax.shard_map(shards, mesh=mesh, in_specs=in_specs, out_specs=out_specs, check_vma=False)
```

profile of v0, /device:TPU:0, one launch (start us, length us, event | category | flops | bytes accessed | tf_op | source)
XLA Modules:
  0.0 1759.0 jit_solution(16797219213902656720)
XLA Ops:
  17.9 79.2 %all-reduce.10 = (bf16[128]{0:T(256)(128)(2,1)S(1)}, bf16[1536]{0:T(1024)(128)(2,1)S(1)}, bf16[128]{0:T(256)(128)(2,1)S(1)}, bf16[768]{0:T(1024)(128)(2,1)S(1)}, bf16[1536]{0:T(1024)(128)(2,1)}) all-reduce(bf16[128]{0:T(256)(128)(2,1)S(1)} %dynamic-update-slice.1, ...), channel_id=1, replica_groups=mesh['dp'=16,'tensor'=2] {'dp'}, use_global_device_ids=true, to_apply=%add.1 | all-reduce | flops 4096 | bytes 16384
  97.1 1.4 fusion.12
  98.5 39.9 %all_gather.53 = bf16[128,1536]{1,0:T(8,128)(2,1)S(1)} all-gather(bf16[8,1536]{1,0:T(8,128)(2,1)} %param.20), channel_id=1, replica_groups=mesh['dp'=16,'tensor'=2] {'dp'}, dimensions={0}, use_global_device_ids=true | all-gather | bytes 417792 | tf_op jit(solution)/shard_map/all_gather | solution.py:109
  140.9 39.7 %all_gather.51 = bf16[128,1536]{1,0:T(8,128)(2,1)S(1)} all-gather(bf16[8,1536]{1,0:T(8,128)(2,1)S(1)} %copy-done.36), channel_id=1, replica_groups=mesh['dp'=16,'tensor'=2] {'dp'}, dimensions={0}, use_global_device_ids=true | all-gather | bytes 417792 | tf_op jit(solution)/shard_map/all_gather | solution.py:111
  182.4 2.5 convolution_add_fusion.3
  189.2 3.6 fusion.57
  195.7 13.5 all-reduce.16.cloned.1.call-done
  209.2 1.9 multiply_reduce_fusion.2
  212.7 162.9 %all-gather.12.cloned.1.call-done = bf16[4480,1536]{1,0:T(8,128)(2,1)} async-done(((bf16[280,1536]{1,0:T(8,128)(2,1)}), bf16[4480,1536]{1,0:T(8,128)(2,1)}) %all-gather.12.cloned.1.call-update) | async-done | bytes 13762576 | tf_op jit(solution)/shard_map/all_gather | solution.py:167
  375.6 11.1 fusion.58
  386.7 152.3 %all-gather.14.cloned.1.call-done = bf16[4480,1536]{1,0:T(8,128)(2,1)} async-done(((bf16[280,1536]{1,0:T(8,128)(2,1)}), bf16[4480,1536]{1,0:T(8,128)(2,1)}) %all-gather.14.cloned.1.call-update) | async-done | bytes 13762576 | tf_op jit(solution)/shard_map/all_gather | solution.py:168
  539.0 11.1 fusion.59
  550.1 152.3 %all-gather.16.cloned.1.call-done = bf16[4480,1536]{1,0:T(8,128)(2,1)} async-done(((bf16[280,1536]{1,0:T(8,128)(2,1)}), bf16[4480,1536]{1,0:T(8,128)(2,1)}) %all-gather.16.cloned.1.call-update) | async-done | bytes 13762576 | tf_op jit(solution)/shard_map/all_gather | solution.py:169
  702.4 11.3 multiply_convert_fusion
  713.7 8.7 fusion.60
  722.5 8.4 convolution_add_fusion.2
  731.2 1.7 multiply_cosine_fusion
  732.8 11.1 convolution_convert_fusion
  743.9 5.7 all-reduce.18.cloned.1.call-done
  749.6 2.6 multiply_reduce_fusion
  754.5 1.6 convolution_convert_fusion.1
  756.1 1.9 copy.95
  758.0 1.5 fusion.13
  770.3 1.3 fusion.45
  773.1 3.1 fusion.47
  776.3 4.3 copy.100
  780.6 6.8 all-to-all-start
  787.4 4.4 copy.102
  791.8 59.0 %all-to-all-done = bf16[256,16,280]{0,2,1:T(8,128)(2,1)} async-done(((bf16[256,16,280]{0,2,1:T(8,128)(2,1)}), bf16[256,16,280]{0,2,1:T(8,128)(2,1)}, u32[]{:S(2)}, u32[]{:S(2)}) %all-to-all-start) | async-done | bytes 2293792 | tf_op jit(solution)/shard_map/all_to_all | solution.py:197
  850.8 22.3 %all-to-all-start.1 = ((bf16[256,16,280]{0,2,1:T(8,128)(2,1)}), bf16[256,16,280]{0,2,1:T(8,128)(2,1)}, u32[]{:S(2)}, u32[]{:S(2)}) async-start(bf16[256,16,280]{0,2,1:T(8,128)(2,1)} %bitcast.157), calls=%async_computation.5 | async-start | bytes 4587520 | tf_op jit(solution)/shard_map/all_to_all | solution.py:198
  873.1 4.3 fusion.29
  877.4 4.2 copy.104
  881.7 51.8 %all-to-all-done.1 = bf16[256,16,280]{0,2,1:T(8,128)(2,1)} async-done(((bf16[256,16,280]{0,2,1:T(8,128)(2,1)}), bf16[256,16,280]{0,2,1:T(8,128)(2,1)}, u32[]{:S(2)}, u32[]{:S(2)}) %all-to-all-start.1) | async-done | bytes 2293792 | tf_op jit(solution)/shard_map/all_to_all | solution.py:198
  933.4 37.2 %all-to-all-start.2 = ((bf16[256,16,280]{0,2,1:T(8,128)(2,1)}), bf16[256,16,280]{0,2,1:T(8,128)(2,1)}, u32[]{:S(2)}, u32[]{:S(2)}) async-start(bf16[256,16,280]{0,2,1:T(8,128)(2,1)} %bitcast.156), calls=%async_computation.6 | async-start | bytes 4587520 | tf_op jit(solution)/shard_map/all_to_all | solution.py:199
  972.6 1.9 fusion.11
  974.5 138.6 %all-reduce.9 = (f32[1536]{0:T(1024)S(1)}, f32[768]{0:T(1024)S(1)}, f32[128]{0:T(128)}, f32[128]{0:T(128)S(1)}, f32[1536]{0:T(1024)S(1)}) all-reduce(f32[1536]{0:T(1024)S(1)} %get-tuple-element.67, f32[768]{0:T(1024)S(1)} %bitcast.172, f32[128]{0:T(128)S(1)} %copy-done.43, ...), channel_id=2, replica_groups=mesh['dp'=16,'tensor'=2] {'dp'}, use_global_device_ids=true, to_apply=%region_15.16.clone | all-reduce | flops 4096 | bytes 32768
  1115.4 3.7 fusion.8
  1119.2 3.5 copy.116
  1122.6 1.9 copy.117
  1124.5 3.3 copy.118
  1127.9 10.3 fusion.62
  1138.2 5.0 fusion.63
  1143.2 67.4 %all-gather.20.cloned.1.call-done = bf16[4096,1536]{1,0:T(8,128)(2,1)} async-done(((bf16[256,1536]{1,0:T(8,128)(2,1)}), bf16[4096,1536]{1,0:T(8,128)(2,1)}) %all-gather.20.cloned.1.call-update) | async-done | bytes 12582928 | tf_op jit(solution)/shard_map/all_gather | solution.py:202
  1210.6 10.2 fusion.64
  1220.8 117.2 %reduce-scatter.7.cloned.1.call-done = f32[8,1536]{1,0:T(8,128)} async-done(((f32[128,1536]{1,0:T(8,128)}), f32[8,1536]{1,0:T(8,128)}) %reduce-scatter.7.cloned.1.call-update) | async-done | bytes 49168 | tf_op jit(solution)/shard_map/reduce_scatter | solution.py:294
  1338.0 128.0 %reduce-scatter.9.cloned.1.call-done = f32[8,1536]{1,0:T(8,128)} async-done(((f32[128,1536]{1,0:T(8,128)}), f32[8,1536]{1,0:T(8,128)}) %reduce-scatter.9.cloned.1.call-update) | async-done | bytes 49168 | tf_op jit(solution)/shard_map/reduce_scatter | solution.py:295
  1466.0 143.4 %reduce-scatter.5.cloned.1.call-done = f32[48,1536]{1,0:T(8,128)} async-done(((f32[768,1536]{1,0:T(8,128)}), f32[48,1536]{1,0:T(8,128)}) %reduce-scatter.5.cloned.1.call-update) | async-done | bytes 294928 | tf_op jit(solution)/shard_map/reduce_scatter | solution.py:292
  1609.4 142.8 %reduce-scatter.11.cloned.1.call-done = f32[48,1536]{1,0:T(8,128)} async-done(((f32[768,1536]{1,0:T(8,128)}), f32[48,1536]{1,0:T(8,128)}) %reduce-scatter.11.cloned.1.call-update) | async-done | bytes 294928 | tf_op jit(solution)/shard_map/reduce_scatter | solution.py:297
  (186 shorter events, 38.5 us)
Async XLA Ops:
  7.2 131.5 %copy-start = (bf16[256,1536]{1,0:T(8,128)(2,1)S(1)}, bf16[256,1536]{1,0:T(8,128)(2,1)}, u32[]{:S(2)}) copy-start(bf16[256,1536]{1,0:T(8,128)(2,1)} %param.15) | copy-start | bytes 2359300
  7.2 175.2 %all-gather.8.cloned.1.call-start = ((), (), s32[]{:S(2)}) async-start(), calls=%async_computation.7 | async-start | bytes 2506752 | tf_op jit(solution)/shard_map/all_gather | solution.py:107
  7.9 181.2 %all-gather.10.cloned.1.call-start = ((), (), s32[]{:S(2)}) async-start(), calls=%async_computation.8 | async-start | bytes 2506752 | tf_op jit(solution)/shard_map/all_gather | solution.py:113
  8.7 200.5 %all-reduce.16.cloned.1.call-start = ((), (), s32[]{:S(2)}) async-start(), calls=%async_computation.9 | async-start | bytes 3145728 | tf_op jit(solution)/shard_map/psum | solution.py:163
  10.4 128.8 %copy-start.41 = (f32[64]{0:T(128)}, f32[64]{0:T(128)S(1)}, u32[]{:S(2)}) copy-start(f32[64]{0:T(128)S(1)} %multiply_power_fusion) | copy-start | bytes 772
  138.4 44.0 %copy-start.33 = (f32[256]{0:T(256)}, f32[256]{0:T(256)S(1)}, u32[]{:S(2)}) copy-start(f32[256]{0:T(256)S(1)} %add_rsqrt_fusion.1) | copy-start | bytes 3076
  139.2 1.7 copy-start.36
  139.9 45.4 %copy-start.21 = (f32[256,128]{0,1:T(8,128)}, f32[256,128]{0,1:T(8,128)S(1)}, u32[]{:S(2)}) copy-start(f32[256,128]{0,1:T(8,128)S(1)} %get-tuple-element.114) | copy-start | bytes 393220
  180.6 4.3 copy-start.19
  187.1 1.6 copy-start.28
  192.8 2.3 copy-start.40
  192.8 182.8 %all-gather.12.cloned.1.call-start = ((), (), s32[]{:S(2)}) async-start(), calls=%async_computation.10 | async-start | bytes 14622720 | tf_op jit(solution)/shard_map/all_gather | solution.py:167
  193.4 345.6 %all-gather.14.cloned.1.call-start = ((), (), s32[]{:S(2)}) async-start(), calls=%async_computation.11 | async-start | bytes 14622720 | tf_op jit(solution)/shard_map/all_gather | solution.py:168
  194.0 508.5 %all-gather.16.cloned.1.call-start = ((), (), s32[]{:S(2)}) async-start(), calls=%async_computation.12 | async-start | bytes 14622720 | tf_op jit(solution)/shard_map/all_gather | solution.py:169
  194.5 555.1 %all-reduce.18.cloned.1.call-start = ((), (), s32[]{:S(2)}) async-start(), calls=%async_computation.13 | async-start | bytes 3145728 | tf_op jit(solution)/shard_map/psum | solution.py:195
  209.2 2.5 copy-start.31
  713.7 8.8 copy-start.16
  713.7 8.8 copy-start.15
  730.9 241.7 %all-reduce.20.cloned.1.call-start = ((), (), s32[]{:S(2)}) async-start(), calls=%async_computation.20 | async-start | bytes 3145728 | tf_op jit(solution)/shard_map/psum | solution.py:174
  749.6 2.6 copy-start.8
  749.6 2.6 copy-start.12
  749.6 2.6 copy-start.32
  749.6 2.6 copy-start.38
  752.3 2.2 copy-start.3
  758.0 1.5 copy-start.9
  760.5 6.5 copy-start.25
  762.6 1.4 copy-start.7
  762.6 1.4 copy-start.29
  762.7 1.7 copy-start.30
  763.9 1.7 copy-start.14
  768.9 1.4 copy-start.1
  768.9 1.4 copy-start.24
  768.9 1.4 copy-start.34
  768.9 359.0 %all-gather.18.cloned.1.call-start = ((), (), s32[]{:S(2)}) async-start(), calls=%async_computation.18 | async-start | bytes 13369344 | tf_op jit(solution)/shard_map/all_gather | solution.py:201
  769.6 2.1 copy-start.26
  769.7 440.9 %all-gather.20.cloned.1.call-start = ((), (), s32[]{:S(2)}) async-start(), calls=%async_computation.19 | async-start | bytes 13369344 | tf_op jit(solution)/shard_map/all_gather | solution.py:202
  770.2 567.7 %reduce-scatter.7.cloned.1.call-start = ((), (), s32[]{:S(2)}) async-start(), calls=%async_computation.15 | async-start | bytes 835584 | tf_op jit(solution)/shard_map/reduce_scatter | solution.py:294
  771.7 694.4 %reduce-scatter.9.cloned.1.call-start = ((), (), s32[]{:S(2)}) async-start(), calls=%async_computation.16 | async-start | bytes 835584 | tf_op jit(solution)/shard_map/reduce_scatter | solution.py:295
  773.1 836.3 %reduce-scatter.5.cloned.1.call-start = ((), (), s32[]{:S(2)}) async-start(), calls=%async_computation.14 | async-start | bytes 5013504 | tf_op jit(solution)/shard_map/reduce_scatter | solution.py:292
  780.6 70.2 %all-to-all-start = ((bf16[256,16,280]{0,2,1:T(8,128)(2,1)}), bf16[256,16,280]{0,2,1:T(8,128)(2,1)}, u32[]{:S(2)}, u32[]{:S(2)}) async-start(bf16[256,16,280]{0,2,1:T(8,128)(2,1)} %bitcast.158), calls=%async_computation.4 | async-start | bytes 4587520 | tf_op jit(solution)/shard_map/all_to_all | solution.py:197
  850.8 82.7 %all-to-all-start.1 = ((bf16[256,16,280]{0,2,1:T(8,128)(2,1)}), bf16[256,16,280]{0,2,1:T(8,128)(2,1)}, u32[]{:S(2)}, u32[]{:S(2)}) async-start(bf16[256,16,280]{0,2,1:T(8,128)(2,1)} %bitcast.157), calls=%async_computation.5 | async-start | bytes 4587520 | tf_op jit(solution)/shard_map/all_to_all | solution.py:198
  873.0 879.2 %reduce-scatter.11.cloned.1.call-start = ((), (), s32[]{:S(2)}) async-start(), calls=%async_computation.17 | async-start | bytes 5013504 | tf_op jit(solution)/shard_map/reduce_scatter | solution.py:297
  933.4 191.1 %all-to-all-start.2 = ((bf16[256,16,280]{0,2,1:T(8,128)(2,1)}), bf16[256,16,280]{0,2,1:T(8,128)(2,1)}, u32[]{:S(2)}, u32[]{:S(2)}) async-start(bf16[256,16,280]{0,2,1:T(8,128)(2,1)} %bitcast.156), calls=%async_computation.6 | async-start | bytes 4587520 | tf_op jit(solution)/shard_map/all_to_all | solution.py:199
  970.6 3.9 copy-start.35
  970.6 3.9 copy-start.42
  970.6 3.9 copy-start.43
  972.6 142.8 %copy-start.13 = (bf16[256,1536]{1,0:T(8,128)(2,1)S(1)}, bf16[256,1536]{1,0:T(8,128)(2,1)}, u32[]{:S(2)}) copy-start(bf16[256,1536]{1,0:T(8,128)(2,1)} %get-tuple-element.94) | copy-start | bytes 2359300
  1127.9 10.3 copy-start.44
  (14 other events, 12.5 us)
Sparse Core Ops, SparseCore 0:
  10.8 65.3 all-gather.7
  79.0 64.5 all-gather.9
  192.9 16.2 all-reduce.15
  211.8 163.7 all-gather.11
  378.2 160.7 all-gather.13
  541.7 160.7 all-gather.15
  731.1 18.5 all-reduce.17
  769.0 21.6 all-reduce.19
  794.1 261.4 all-gather.17
  1058.2 152.3 all-gather.19
  1215.9 122.0 reduce-scatter.6
  1343.1 122.8 reduce-scatter.8
  1471.8 137.5 reduce-scatter.4
  1615.0 137.1 reduce-scatter.10
where the time goes:
time: 1770 us; the launch traced here: 1760 us
  waiting for transfers between devices  1200 us (68%)
  blocking collectives  297 us (17%)
  matrix products  114 us (6%)
  starting transfers between devices  67.4 us (4%)
  local copies, waits for them, and re-layouts  41.1 us (2%)
  other arithmetic  19.8 us (1%)
  between operations  18.7 us (1%)
    unnamed x2, blocking collectives  218 us
    all_gather x1, waiting for transfers between devices, shards(): piece_gate = lax.all_gather(w_gate, 'dp', axis=0, tiled=True)  163 us
    all_gather x1, waiting for transfers between devices, shards(): piece_up = lax.all_gather(w_up, 'dp', axis=0, tiled=True)  152 us
    all_gather x1, waiting for transfers between devices, shards(): piece_down = lax.all_gather(w_down, 'dp', axis=0, tiled=True)  152 us
    reduce_scatter x1, waiting for transfers between devices, shards(): lax.psum_scatter(grad_query_weight, 'dp', scatter_dimension=0, tiled=True)  143 us
    reduce_scatter x1, waiting for transfers between devices, shards(): lax.psum_scatter(grad_out_weight, 'dp', scatter_dimension=0, tiled=True)  143 us
    reduce_scatter x1, waiting for transfers between devices, shards(): lax.psum_scatter(grad_value_weight, 'dp', scatter_dimension=0, tiled=True)  128 us
    reduce_scatter x1, waiting for transfers between devices, shards(): lax.psum_scatter(grad_key_weight, 'dp', scatter_dimension=0, tiled=True)  117 us
  transfers between devices with their start and end apart: 17, of which 12 were waited for; matrix products, arithmetic and copies ran while one was open for 7% of the time, Pallas kernels for 0%

commit v1 on v0

--- a/solution.py
+++ b/solution.py
@@ -196,7 +196,12 @@
     traded = (
         lax.all_to_all(gate_grads, "dp", split_axis=1, concat_axis=0, tiled=True),
         lax.all_to_all(up_grads, "dp", split_axis=1, concat_axis=0, tiled=True),
-        lax.all_to_all(hidden_all, "dp", split_axis=1, concat_axis=0, tiled=True),
+        jnp.concatenate(
+            lax.all_to_all(
+                jnp.stack(jnp.split(hidden_all, lax.axis_size("dp"), axis=1)), "dp", 0, 0
+            ),
+            axis=0,
+        ),
     )
     piece_second = lax.all_gather(second_low, "dp", axis=0, tiled=True)
     piece_grad = lax.all_gather(grad_out, "dp", axis=0, tiled=True)

time: 1770 us -> 1770 us (level)
  waiting for transfers between devices: 1200 us -> 1170 us
  local copies, waits for them, and re-layouts: 41.1 us -> 70.6 us
    all_to_all x1, waiting for transfers between devices: 51.8 us -> 24.7 us  [shards(): lax.all_to_all(up_grads, 'dp', split_axis=1, concat_axis=0, tiled=True)]
    unnamed x105 -> x120, local copies, waits for them, and re-layouts: 15.8 us -> 41.1 us
  transfers between devices with their start and end apart: 17 -> 17, of which waited for: 12 -> 12; matrix products, arithmetic and copies ran while one was open for 7% -> 9% of each run, Pallas kernels for 0% -> 0%
where the time goes in v1:
time: 1770 us; the launch traced here: 1760 us
  waiting for transfers between devices  1170 us (66%)
  blocking collectives  298 us (17%)
  matrix products  114 us (6%)
  local copies, waits for them, and re-layouts  70.6 us (4%)
  starting transfers between devices  67.3 us (4%)
  other arithmetic  20.5 us (1%)
  between operations  18.7 us (1%)
    unnamed x2, blocking collectives  218 us
    all_gather x1, waiting for transfers between devices, shards(): piece_gate = lax.all_gather(w_gate, 'dp', axis=0, tiled=True)  163 us
    all_gather x1, waiting for transfers between devices, shards(): piece_up = lax.all_gather(w_up, 'dp', axis=0, tiled=True)  152 us
    all_gather x1, waiting for transfers between devices, shards(): piece_down = lax.all_gather(w_down, 'dp', axis=0, tiled=True)  152 us
    reduce_scatter x1, waiting for transfers between devices, shards(): lax.psum_scatter(grad_query_weight, 'dp', scatter_dimension=0, tiled=True)  144 us
    reduce_scatter x1, waiting for transfers between devices, shards(): lax.psum_scatter(grad_out_weight, 'dp', scatter_dimension=0, tiled=True)  143 us
    reduce_scatter x1, waiting for transfers between devices, shards(): lax.psum_scatter(grad_value_weight, 'dp', scatter_dimension=0, tiled=True)  128 us
    reduce_scatter x1, waiting for transfers between devices, shards(): lax.psum_scatter(grad_key_weight, 'dp', scatter_dimension=0, tiled=True)  117 us
  transfers between devices with their start and end apart: 17, of which 12 were waited for; matrix products, arithmetic and copies ran while one was open for 9% of the time, Pallas kernels for 0%

profile of v1, /device:TPU:0, one launch (start us, length us, event | category | flops | bytes accessed | tf_op | source)
XLA Modules:
  0.0 1760.5 jit_solution(16412283652838006506)
XLA Ops:
  17.9 79.2 %all-reduce.10 = (bf16[128]{0:T(256)(128)(2,1)S(1)}, bf16[1536]{0:T(1024)(128)(2,1)S(1)}, bf16[128]{0:T(256)(128)(2,1)S(1)}, bf16[768]{0:T(1024)(128)(2,1)S(1)}, bf16[1536]{0:T(1024)(128)(2,1)}) all-reduce(bf16[128]{0:T(256)(128)(2,1)S(1)} %dynamic-update-slice.1, ...), channel_id=1, replica_groups=mesh['dp'=16,'tensor'=2] {'dp'}, use_global_device_ids=true, to_apply=%add.1 | all-reduce | flops 4096 | bytes 16384
  98.5 39.6 %all_gather.53 = bf16[128,1536]{1,0:T(8,128)(2,1)S(1)} all-gather(bf16[8,1536]{1,0:T(8,128)(2,1)} %param.20), channel_id=1, replica_groups=mesh['dp'=16,'tensor'=2] {'dp'}, dimensions={0}, use_global_device_ids=true | all-gather | bytes 417792 | tf_op jit(solution)/shard_map/all_gather | solution.py:109
  141.5 40.0 %all_gather.51 = bf16[128,1536]{1,0:T(8,128)(2,1)S(1)} all-gather(bf16[8,1536]{1,0:T(8,128)(2,1)S(1)} %copy-done.37), channel_id=1, replica_groups=mesh['dp'=16,'tensor'=2] {'dp'}, dimensions={0}, use_global_device_ids=true | all-gather | bytes 417792 | tf_op jit(solution)/shard_map/all_gather | solution.py:111
  183.3 2.5 convolution_add_fusion.3
  190.9 3.6 fusion.73
  197.4 13.5 all-reduce.16.cloned.1.call-done
  210.9 1.9 multiply_reduce_fusion.2
  214.5 162.9 %all-gather.12.cloned.1.call-done = bf16[4480,1536]{1,0:T(8,128)(2,1)} async-done(((bf16[280,1536]{1,0:T(8,128)(2,1)}), bf16[4480,1536]{1,0:T(8,128)(2,1)}) %all-gather.12.cloned.1.call-update) | async-done | bytes 13762576 | tf_op jit(solution)/shard_map/all_gather | solution.py:167
  377.3 11.1 fusion.74
  388.4 152.3 %all-gather.14.cloned.1.call-done = bf16[4480,1536]{1,0:T(8,128)(2,1)} async-done(((bf16[280,1536]{1,0:T(8,128)(2,1)}), bf16[4480,1536]{1,0:T(8,128)(2,1)}) %all-gather.14.cloned.1.call-update) | async-done | bytes 13762576 | tf_op jit(solution)/shard_map/all_gather | solution.py:168
  540.8 11.1 fusion.75
  551.9 152.3 %all-gather.16.cloned.1.call-done = bf16[4480,1536]{1,0:T(8,128)(2,1)} async-done(((bf16[280,1536]{1,0:T(8,128)(2,1)}), bf16[4480,1536]{1,0:T(8,128)(2,1)}) %all-gather.16.cloned.1.call-update) | async-done | bytes 13762576 | tf_op jit(solution)/shard_map/all_gather | solution.py:169
  704.2 11.3 multiply_convert_fusion
  715.5 8.7 fusion.76
  724.3 8.4 convolution_add_fusion.2
  734.5 11.1 convolution_convert_fusion
  745.6 5.8 all-reduce.18.cloned.1.call-done
  751.4 2.6 multiply_reduce_fusion
  757.8 1.9 copy.112
  773.7 3.1 fusion.63
  776.9 4.3 copy.117
  781.1 6.8 all-to-all-start
  788.0 4.3 copy.119
  792.3 59.0 %all-to-all-done = bf16[256,16,280]{0,2,1:T(8,128)(2,1)} async-done(((bf16[256,16,280]{0,2,1:T(8,128)(2,1)}), bf16[256,16,280]{0,2,1:T(8,128)(2,1)}, u32[]{:S(2)}, u32[]{:S(2)}) %all-to-all-start) | async-done | bytes 2293792 | tf_op jit(solution)/shard_map/all_to_all | solution.py:197
  851.4 22.3 %all-to-all-start.1 = ((bf16[256,16,280]{0,2,1:T(8,128)(2,1)}), bf16[256,16,280]{0,2,1:T(8,128)(2,1)}, u32[]{:S(2)}, u32[]{:S(2)}) async-start(bf16[256,16,280]{0,2,1:T(8,128)(2,1)} %bitcast.218), calls=%async_computation.5 | async-start | bytes 4587520 | tf_op jit(solution)/shard_map/all_to_all | solution.py:198
  879.2 1.8 fusion.48
  880.9 1.8 fusion.47
  882.7 1.8 fusion.46
  887.9 2.9 fusion.29
  890.9 1.8 fusion.43
  897.9 1.8 fusion.39
  904.8 4.5 copy.121
  909.4 24.7 %all-to-all-done.1 = bf16[256,16,280]{0,2,1:T(8,128)(2,1)} async-done(((bf16[256,16,280]{0,2,1:T(8,128)(2,1)}), bf16[256,16,280]{0,2,1:T(8,128)(2,1)}, u32[]{:S(2)}, u32[]{:S(2)}) %all-to-all-start.1) | async-done | bytes 2293792 | tf_op jit(solution)/shard_map/all_to_all | solution.py:198
  934.0 36.7 %all-to-all-start.2 = ((bf16[16,256,280]{1,2,0:T(8,128)(2,1)}), bf16[16,256,280]{1,2,0:T(8,128)(2,1)}, u32[]{:S(2)}, u32[]{:S(2)}) async-start(bf16[16,256,280]{1,2,0:T(8,128)(2,1)} %copy.121), calls=%async_computation.6 | async-start | bytes 4587520 | tf_op jit(solution)/shard_map/all_to_all | solution.py:200
  972.7 1.8 fusion.11
  974.6 139.1 %all-reduce.9 = (f32[1536]{0:T(1024)S(1)}, f32[768]{0:T(1024)S(1)}, f32[128]{0:T(128)}, f32[128]{0:T(128)S(1)}, f32[1536]{0:T(1024)S(1)}) all-reduce(f32[1536]{0:T(1024)S(1)} %get-tuple-element.67, f32[768]{0:T(1024)S(1)} %bitcast.233, f32[128]{0:T(128)S(1)} %get-tuple-element.95, ...), channel_id=2, replica_groups=mesh['dp'=16,'tensor'=2] {'dp'}, use_global_device_ids=true, to_apply=%region_15.16.clone | all-reduce | flops 4096 | bytes 32768
  1116.0 3.9 fusion.8
  1120.0 3.4 copy.133
  1123.4 3.3 copy.134
  1126.7 3.3 copy.135
  1130.0 10.3 fusion.78
  1141.5 5.0 fusion.79
  1146.5 64.7 %all-gather.20.cloned.1.call-done = bf16[4096,1536]{1,0:T(8,128)(2,1)} async-done(((bf16[256,1536]{1,0:T(8,128)(2,1)}), bf16[4096,1536]{1,0:T(8,128)(2,1)}) %all-gather.20.cloned.1.call-update) | async-done | bytes 12582928 | tf_op jit(solution)/shard_map/all_gather | solution.py:207
  1211.2 10.2 fusion.80
  1221.4 117.2 %reduce-scatter.7.cloned.1.call-done = f32[8,1536]{1,0:T(8,128)} async-done(((f32[128,1536]{1,0:T(8,128)}), f32[8,1536]{1,0:T(8,128)}) %reduce-scatter.7.cloned.1.call-update) | async-done | bytes 49168 | tf_op jit(solution)/shard_map/reduce_scatter | solution.py:299
  1338.6 127.9 %reduce-scatter.9.cloned.1.call-done = f32[8,1536]{1,0:T(8,128)} async-done(((f32[128,1536]{1,0:T(8,128)}), f32[8,1536]{1,0:T(8,128)}) %reduce-scatter.9.cloned.1.call-update) | async-done | bytes 49168 | tf_op jit(solution)/shard_map/reduce_scatter | solution.py:300
  1466.5 144.1 %reduce-scatter.5.cloned.1.call-done = f32[48,1536]{1,0:T(8,128)} async-done(((f32[768,1536]{1,0:T(8,128)}), f32[48,1536]{1,0:T(8,128)}) %reduce-scatter.5.cloned.1.call-update) | async-done | bytes 294928 | tf_op jit(solution)/shard_map/reduce_scatter | solution.py:297
  1610.6 143.1 %reduce-scatter.11.cloned.1.call-done = f32[48,1536]{1,0:T(8,128)} async-done(((f32[768,1536]{1,0:T(8,128)}), f32[48,1536]{1,0:T(8,128)}) %reduce-scatter.11.cloned.1.call-update) | async-done | bytes 294928 | tf_op jit(solution)/shard_map/reduce_scatter | solution.py:302
  (202 shorter events, 66.9 us)
Async XLA Ops:
  7.2 176.1 %all-gather.8.cloned.1.call-start = ((), (), s32[]{:S(2)}) async-start(), calls=%async_computation.7 | async-start | bytes 2506752 | tf_op jit(solution)/shard_map/all_gather | solution.py:107
  7.9 183.0 %all-gather.10.cloned.1.call-start = ((), (), s32[]{:S(2)}) async-start(), calls=%async_computation.8 | async-start | bytes 2506752 | tf_op jit(solution)/shard_map/all_gather | solution.py:113
  8.7 202.3 %all-reduce.16.cloned.1.call-start = ((), (), s32[]{:S(2)}) async-start(), calls=%async_computation.9 | async-start | bytes 3145728 | tf_op jit(solution)/shard_map/psum | solution.py:163
  10.4 127.8 %copy-start.42 = (f32[64]{0:T(128)}, f32[64]{0:T(128)S(1)}, u32[]{:S(2)}) copy-start(f32[64]{0:T(128)S(1)} %multiply_power_fusion) | copy-start | bytes 772
  138.1 45.2 %copy-start.34 = (f32[256]{0:T(256)}, f32[256]{0:T(256)S(1)}, u32[]{:S(2)}) copy-start(f32[256]{0:T(256)S(1)} %add_rsqrt_fusion.1) | copy-start | bytes 3076
  138.2 2.3 copy-start.40
  138.9 2.6 copy-start.37
  140.5 41.0 %copy-start = (bf16[256,1536]{1,0:T(8,128)(2,1)S(1)}, bf16[256,1536]{1,0:T(8,128)(2,1)}, u32[]{:S(2)}) copy-start(bf16[256,1536]{1,0:T(8,128)(2,1)} %param.15) | copy-start | bytes 2359300
  141.2 41.4 %copy-start.11 = (f32[256,128]{0,1:T(8,128)}, f32[256,128]{0,1:T(8,128)S(1)}, u32[]{:S(2)}) copy-start(f32[256,128]{0,1:T(8,128)S(1)} %get-tuple-element.112) | copy-start | bytes 393220
  141.2 45.0 %copy-start.22 = (f32[256,128]{0,1:T(8,128)}, f32[256,128]{0,1:T(8,128)S(1)}, u32[]{:S(2)}) copy-start(f32[256,128]{0,1:T(8,128)S(1)} %get-tuple-element.114) | copy-start | bytes 393220
  181.5 4.3 copy-start.20
  186.2 2.7 copy-start.7
  188.7 1.7 copy-start.29
  194.5 2.3 copy-start.41
  194.5 182.8 %all-gather.12.cloned.1.call-start = ((), (), s32[]{:S(2)}) async-start(), calls=%async_computation.10 | async-start | bytes 14622720 | tf_op jit(solution)/shard_map/all_gather | solution.py:167
  195.1 345.7 %all-gather.14.cloned.1.call-start = ((), (), s32[]{:S(2)}) async-start(), calls=%async_computation.11 | async-start | bytes 14622720 | tf_op jit(solution)/shard_map/all_gather | solution.py:168
  195.7 508.5 %all-gather.16.cloned.1.call-start = ((), (), s32[]{:S(2)}) async-start(), calls=%async_computation.12 | async-start | bytes 14622720 | tf_op jit(solution)/shard_map/all_gather | solution.py:169
  196.3 555.1 %all-reduce.18.cloned.1.call-start = ((), (), s32[]{:S(2)}) async-start(), calls=%async_computation.13 | async-start | bytes 3145728 | tf_op jit(solution)/shard_map/psum | solution.py:195
  210.9 2.5 copy-start.32
  715.5 8.8 copy-start.16
  715.5 8.8 copy-start.15
  732.7 240.0 %all-reduce.20.cloned.1.call-start = ((), (), s32[]{:S(2)}) async-start(), calls=%async_computation.20 | async-start | bytes 3145728 | tf_op jit(solution)/shard_map/psum | solution.py:174
  751.4 2.6 copy-start.9
  751.4 2.6 copy-start.13
  751.4 2.6 copy-start.33
  751.4 2.6 copy-start.39
  754.0 2.2 copy-start.4
  762.3 5.3 copy-start.26
  764.3 1.6 copy-start.31
  764.3 2.0 copy-start.14
  768.1 2.7 copy-start.1
  768.1 2.7 copy-start.25
  768.1 2.7 copy-start.35
  769.4 2.8 copy-start.27
  769.5 360.6 %all-gather.18.cloned.1.call-start = ((), (), s32[]{:S(2)}) async-start(), calls=%async_computation.18 | async-start | bytes 13369344 | tf_op jit(solution)/shard_map/all_gather | solution.py:206
  770.2 441.0 %all-gather.20.cloned.1.call-start = ((), (), s32[]{:S(2)}) async-start(), calls=%async_computation.19 | async-start | bytes 13369344 | tf_op jit(solution)/shard_map/all_gather | solution.py:207
  770.8 567.8 %reduce-scatter.7.cloned.1.call-start = ((), (), s32[]{:S(2)}) async-start(), calls=%async_computation.15 | async-start | bytes 835584 | tf_op jit(solution)/shard_map/reduce_scatter | solution.py:299
  772.2 694.2 %reduce-scatter.9.cloned.1.call-start = ((), (), s32[]{:S(2)}) async-start(), calls=%async_computation.16 | async-start | bytes 835584 | tf_op jit(solution)/shard_map/reduce_scatter | solution.py:300
  773.7 836.9 %reduce-scatter.5.cloned.1.call-start = ((), (), s32[]{:S(2)}) async-start(), calls=%async_computation.14 | async-start | bytes 5013504 | tf_op jit(solution)/shard_map/reduce_scatter | solution.py:297
  781.1 70.2 %all-to-all-start = ((bf16[256,16,280]{0,2,1:T(8,128)(2,1)}), bf16[256,16,280]{0,2,1:T(8,128)(2,1)}, u32[]{:S(2)}, u32[]{:S(2)}) async-start(bf16[256,16,280]{0,2,1:T(8,128)(2,1)} %bitcast.219), calls=%async_computation.4 | async-start | bytes 4587520 | tf_op jit(solution)/shard_map/all_to_all | solution.py:197
  851.4 82.7 %all-to-all-start.1 = ((bf16[256,16,280]{0,2,1:T(8,128)(2,1)}), bf16[256,16,280]{0,2,1:T(8,128)(2,1)}, u32[]{:S(2)}, u32[]{:S(2)}) async-start(bf16[256,16,280]{0,2,1:T(8,128)(2,1)} %bitcast.218), calls=%async_computation.5 | async-start | bytes 4587520 | tf_op jit(solution)/shard_map/all_to_all | solution.py:198
  873.7 880.0 %reduce-scatter.11.cloned.1.call-start = ((), (), s32[]{:S(2)}) async-start(), calls=%async_computation.17 | async-start | bytes 5013504 | tf_op jit(solution)/shard_map/reduce_scatter | solution.py:302
  873.9 14.0 copy-start.3
  909.4 65.2 %copy-start.36 = (f32[1536]{0:T(1024)S(1)}, f32[1536]{0:T(1024)}, u32[]{:S(2)}) copy-start(f32[1536]{0:T(1024)} %get-tuple-element.65) | copy-start | bytes 18436
  909.4 65.2 %copy-start.43 = (f32[128]{0:T(128)S(1)}, f32[128]{0:T(128)}, u32[]{:S(2)}) copy-start(f32[128]{0:T(128)} %get-tuple-element.129) | copy-start | bytes 1540
  934.0 192.7 %all-to-all-start.2 = ((bf16[16,256,280]{1,2,0:T(8,128)(2,1)}), bf16[16,256,280]{1,2,0:T(8,128)(2,1)}, u32[]{:S(2)}, u32[]{:S(2)}) async-start(bf16[16,256,280]{1,2,0:T(8,128)(2,1)} %copy.121), calls=%async_computation.6 | async-start | bytes 4587520 | tf_op jit(solution)/shard_map/all_to_all | solution.py:200
  1130.0 10.3 copy-start.17
  1130.0 11.5 copy-start.44
  (14 other events, 15.4 us)
Sparse Core Ops, SparseCore 0:
  10.8 65.3 all-gather.7
  79.0 65.1 all-gather.9
  194.6 16.2 all-reduce.15
  213.6 163.7 all-gather.11
  380.0 160.7 all-gather.13
  543.4 160.7 all-gather.15
  732.8 18.5 all-reduce.17
  769.6 21.5 all-reduce.19
  794.6 261.4 all-gather.17
  1058.7 152.4 all-gather.19
  1216.5 122.0 reduce-scatter.6
  1343.7 122.7 reduce-scatter.8
  1472.2 138.3 reduce-scatter.4
  1616.2 137.4 reduce-scatter.10
